TPU v7x, 32 devices: a whole 2x2x4 slice. The times are simulated.
32 devices in a mesh: vol: 8 (over z, x), nar: 4 (over y, core).
Axes of the slice: x: 2, y: 2, z: 4, core: 2. Of those that a mesh axis runs over, the one named last changes fastest.
Arguments:
- series: bfloat16 [2048, 2048], P(('vol', 'nar')), may hold values from -6 to 6
- send_rows: int32 [8, 4, 16], P('vol', 'nar'), may hold values from -1 to 63, as said below
- bin_counts: int32 [4], replicated, may hold values from 1 to 128, 256 in all
- observer_cells: int32 [2, 512], replicated, may hold values from 0 to 127
Outputs:
- spectra_out: float32 [4, 128, 2, 512], P('nar', 'vol')
Inputs may be any that keep to these rules, and one draw needn't show every extreme that they name: `send_rows`: entry (u, n, k) names the row of device (u, n)'s 64 rows of series for slot k mod 2 bound for the patch owner at vol index k // 2 and nar index n, or is -1 for an empty slot; one device never names a row twice. Nar index m owns bin_counts[m] bins in order, from the sum of the counts before m on; some owner holds exactly 128 bins. `observer_cells`: row 0 holds polar indices, row 1 azimuthal indices.
All inputs are finite; a program needn't handle non-finite values.
Results may differ from a plain program's by a relative error of at most 0.0043.
Values may be sent and summed in bfloat16 or wider, within the bound.
No kernel may reach another device: no remote copies, remote signals or barrier semaphores. Data moves between devices by JAX's collectives and lax.ppermute only.
A program may use at most 64 MiB of HBM per device.

v0:
```python
import math
import jax
import jax.numpy as jnp
from jax import lax
from jax.sharding import PartitionSpec as P

NF = 256
NQ = 4
WAVE_STEP = 0.05


def dft_table(bin_ids, keep_bin, time_len):
    time_steps = jnp.arange(time_len, dtype=jnp.int32)
    frequency = bin_ids + 1
    phase_turns = time_steps[:, None] * frequency[None, :] % time_len
    angle_grid = phase_turns.astype(jnp.float32) * (2.0 * math.pi / time_len)
    dft_grid = jnp.stack([jnp.cos(angle_grid), -jnp.sin(angle_grid)], axis=-1)
    dft_grid = jnp.where(keep_bin[None, :, None], dft_grid, jnp.float32(0.0))
    return dft_grid.reshape(time_len, 2 * bin_ids.shape[0]).astype(jnp.bfloat16)


def positions(point_list):
    beside_all = (point_list * 1597 % 8191).astype(jnp.float32) * (2.0 * math.pi / 8191.0)
    jitter = (point_list * 613 % 127).astype(jnp.float32) * (0.37 / 127.0)
    axial = (point_list // 128).astype(jnp.float32) * 0.5 + jitter
    return (20.0 * jnp.cos(beside_all), 20.0 * jnp.sin(beside_all), axial)


def directions(obs_cells):
    polar_angle = (obs_cells[0].astype(jnp.float32) + 0.5) * (math.pi / 128.0)
    azimuth = obs_cells[1].astype(jnp.float32) * (2.0 * math.pi / 128.0)
    return (
        jnp.sin(polar_angle) * jnp.cos(azimuth),
        jnp.sin(polar_angle) * jnp.sin(azimuth),
        jnp.cos(polar_angle),
    )


def project(facing, place_xyz):
    dotted = facing[0][:, None] * place_xyz[0][None, :] + facing[1][:, None] * place_xyz[1][None, :]
    return dotted + facing[2][:, None] * place_xyz[2][None, :]


def kernels(bin_ids, dotted):
    wavenumber = (bin_ids.astype(jnp.float32) + 1.0) * WAVE_STEP
    phase_grid = wavenumber[:, None, None] * dotted[None]
    return jnp.concatenate([jnp.cos(phase_grid), jnp.sin(phase_grid)], axis=1).astype(jnp.bfloat16)


def combine(products, bin_ids, facing, norm_scale):
    observers = facing[0].shape[0]
    bin_total = bin_ids.shape[0]
    cos_part = products[:, :observers].reshape(bin_total, observers, NQ, 2)
    sine_part = products[:, observers:].reshape(bin_total, observers, NQ, 2)
    real_part = cos_part[..., 0] + sine_part[..., 1]
    imag_part = cos_part[..., 1] - sine_part[..., 0]
    weights = jnp.stack([jnp.ones_like(facing[0]), facing[0], facing[1], facing[2]], axis=-1)
    real_sum = jnp.sum(real_part * weights[None], axis=-1)
    imag_sum = jnp.sum(imag_part * weights[None], axis=-1)
    amplitude = (bin_ids.astype(jnp.float32) + 1.0) * (norm_scale / NF)
    return jnp.stack([-amplitude[:, None] * imag_sum, amplitude[:, None] * real_sum], axis=1)


def apply_green(bin_ids, spec_block, dotted, facing, norm_scale):
    green_grid = kernels(bin_ids, dotted)
    products = jnp.einsum(
        "bxp,bcp->bxc", green_grid, spec_block, preferred_element_type=jnp.float32
    )
    return combine(products, bin_ids, facing, norm_scale)


def per_device(series, send_rows, bin_counts, observer_cells):
    vol_count = lax.axis_size("vol")
    nar_count = lax.axis_size("nar")
    vol_index = lax.axis_index("vol")
    nar_index = lax.axis_index("nar")
    bin_cap = vol_count * max(1, 2 * NF // (nar_count * vol_count))
    time_len = series.shape[1] // NQ
    slot_total = send_rows.shape[2]
    slot_width = slot_total // vol_count
    listing = send_rows.reshape(-1)
    picked = jnp.take(series, jnp.maximum(listing, 0), axis=0)
    packed = jnp.where((listing >= 0)[:, None], picked, jnp.zeros((), series.dtype))
    arrived = lax.all_to_all(packed, "vol", split_axis=0, concat_axis=0, tiled=True)
    starts = jnp.cumsum(bin_counts) - bin_counts
    own_start = starts[nar_index]
    own_count = bin_counts[nar_index]
    dft_scale = 1.0 / math.sqrt(time_len)
    within = jnp.arange(bin_cap, dtype=jnp.int32)
    own_table = dft_table(own_start + within, within < own_count, time_len)
    row_piece = lax.all_gather(arrived, "nar", axis=0, tiled=True)
    rows_here = row_piece.shape[0]
    spectral = jnp.dot(
        row_piece.reshape(rows_here * NQ, time_len), own_table, preferred_element_type=jnp.float32
    )
    spectral = (spectral * dft_scale).astype(jnp.bfloat16).reshape(rows_here, NQ, bin_cap, 2)
    spectra = spectral.transpose(2, 1, 3, 0).reshape(bin_cap, 2 * NQ, rows_here)
    local_points = nar_count * slot_total

    def point_ids(vol_owner, flat_index):
        nar_source = flat_index // slot_total
        remain = flat_index % slot_total
        vol_source = remain // slot_width
        within_slot = remain % slot_width
        return (
            (vol_source * nar_count + nar_source) * vol_count + vol_owner
        ) * slot_width + within_slot

    norm_scale = 1.0 / math.sqrt(vol_count * nar_count * slot_total)
    facing = directions(observer_cells)
    share_rows = bin_cap // vol_count
    regrouped = lax.all_to_all(spectra, "vol", split_axis=0, concat_axis=2, tiled=True)
    bin_ids = own_start + vol_index * share_rows + jnp.arange(share_rows, dtype=jnp.int32)
    span_points = local_points * max(1, vol_count // 8)
    turn_count = vol_count * local_points // span_points

    def add_block(turn_index, running):
        first_point = turn_index * span_points
        spec_block = lax.dynamic_slice_in_dim(regrouped, first_point, span_points, 2)
        flat_index = first_point + jnp.arange(span_points, dtype=jnp.int32)
        point_list = point_ids(flat_index // local_points, flat_index % local_points)
        dotted = project(facing, positions(point_list))
        return running + apply_green(bin_ids, spec_block, dotted, facing, norm_scale)

    result = lax.fori_loop(
        0, turn_count, add_block, jnp.zeros((share_rows, 2, observer_cells.shape[1]), jnp.float32)
    )
    return result.reshape(1, share_rows, 2, result.shape[-1])


def solution(mesh):
    placed = (P(("vol", "nar"), None), P("vol", "nar", None), P(), P())
    return jax.shard_map(
        per_device,
        mesh=mesh,
        in_specs=placed,
        out_specs=P("nar", "vol", None, None),
        check_vma=False,
    )
```

profile of v0, /device:TPU:0, one launch (start us, length us, event | category | flops | bytes accessed | tf_op | source)
XLA Modules:
  0.0 133.8 jit_solution(10418153351370994909)
XLA Ops:
  0.0 0.7 compare_reduce_fusion
  0.7 0.7 maximum_bitcast_fusion
  1.6 0.6 gather_fusion
  2.2 0.8 broadcast_select_fusion.1
  3.0 7.3 %all-to-all-start = ((bf16[8,2,2048]{2,1,0:T(2,128)(2,1)}), bf16[8,2,2048]{2,1,0:T(2,128)(2,1)S(1)}, u32[]{:S(2)}, u32[]{:S(2)}) async-start(bf16[8,2,2048]{2,1,0:T(2,128)(2,1)} %broadcast_select_fusion.1), calls=%async_computation | async-start | bytes 131072 | tf_op jit(solution)/shard_map/all_to_all | solution.py:84
  10.3 0.8 reduce-window.9
  11.1 0.7 bitcast_subtract_fusion
  11.8 1.3 dynamic_slice.18
  13.0 0.7 dynamic_slice.17
  13.7 0.7 add_add_fusion
  14.4 1.1 fusion.36
  15.5 0.6 iota_compare_fusion
  16.2 0.2 copy.26
  16.5 0.7 all-to-all-done
  17.2 5.8 %all_gather.3 = bf16[64,2048]{1,0:T(8,128)(2,1)S(1)} all-gather(bf16[16,2048]{1,0:T(8,128)(2,1)S(1)} %all_to_all.20), channel_id=1, replica_groups=mesh['vol'=8,'nar'=4] {'nar'}, dimensions={0}, use_global_device_ids=true | all-gather | bytes 327680 | tf_op jit(solution)/shard_map/all_gather | solution.py:91
  23.0 0.2 reshape.597
  23.2 0.3 fusion.28
  23.5 10.0 %reshape.598 = bf16[64,4,128,2]{1,0,3,2:T(8,128)(2,1)} reshape(bf16[256,256]{0,1:T(8,128)(2,1)S(1)} %copy.27) | data formatting | bytes 262144 | tf_op jit(solution)/shard_map/reshape | solution.py:96
  33.5 6.2 %copy.28 = bf16[128,4,2,64]{0,3,2,1:T(8,128)(2,1)S(1)} copy(bf16[128,4,2,64]{1,3,2,0:T(8,128)(2,1)} %bitcast.64) | data formatting | bytes 262144 | tf_op jit(solution)/shard_map/transpose | solution.py:97
  39.7 0.2 copy.29
  39.9 0.9 reshape.631
  40.8 5.4 %all-to-all-start.1 = ((bf16[8,2,4096]{2,1,0:T(2,128)(2,1)}), bf16[8,2,4096]{2,1,0:T(2,128)(2,1)S(1)}, u32[]{:S(2)}, u32[]{:S(2)}) async-start(bf16[8,2,4096]{2,1,0:T(2,128)(2,1)} %reshape.631), calls=%async_computation.1 | async-start | bytes 262144 | tf_op jit(solution)/shard_map/all_to_all | solution.py:112
  47.0 6.6 %all-to-all-done.1 = bf16[8,2,4096]{2,1,0:T(2,128)(2,1)S(1)} async-done(((bf16[8,2,4096]{2,1,0:T(2,128)(2,1)}), bf16[8,2,4096]{2,1,0:T(2,128)(2,1)S(1)}, u32[]{:S(2)}, u32[]{:S(2)}) %all-to-all-start.1) | async-done | bytes 131104 | tf_op jit(solution)/shard_map/all_to_all | solution.py:112
  53.7 0.2 reshape.632
  53.9 0.2 copy.30
  54.1 0.2 all_to_all.24
  54.3 78.9 %while.19 = (s32[]{:T(128)}, f32[16,2,512]{2,1,0:T(2,128)S(1)}, f32[512]{0:T(512)S(1)}, f32[512]{0:T(512)S(1)}, f32[512]{0:T(512)S(1)}, /*index=5*/bf16[16,8,512...) while((s32[]{:T(128)}, f32[16,2,512]{2,1,0:T(2,128)S(1)}, ...), condition=%wide.region_4.5_spmd.clone.clone.clone, body=%wide.region_1.4_spmd.clone.clone.clone.sunk | while | flops 22971540 | bytes 8845429 | solution.py:125
  54.6 7.8 %fusion.56 = (bf16[16,512,64]{1,2,0:T(8,128)(2,1)S(1)}, bf16[16,512,64]{1,2,0:T(8,128)(2,1)S(1)}) fusion(f32[512,64]{0,1:T(8,128)S(1)} %multiply_add_fusion.2, f32[16]{0:T(128)S(1)} %fusion.55), kind=kLoop, calls=%fused_computation.5.clone.1 | loop fusion | flops 1572864 | bytes 2228288 | tf_op jit(solution)/shard_map/convert
  62.4 0.4 fusion.57
  62.9 0.1 reshape.635
  63.0 0.1 reshape.636
  63.2 0.3 slice_add_fusion.2
  63.6 0.2 fusion.59
  64.5 7.8 %fusion.56 = (bf16[16,512,64]{1,2,0:T(8,128)(2,1)S(1)}, bf16[16,512,64]{1,2,0:T(8,128)(2,1)S(1)}) fusion(f32[512,64]{0,1:T(8,128)S(1)} %multiply_add_fusion.2, f32[16]{0:T(128)S(1)} %fusion.55), kind=kLoop, calls=%fused_computation.5.clone.1 | loop fusion | flops 1572864 | bytes 2228288 | tf_op jit(solution)/shard_map/convert
  72.2 0.4 fusion.57
  73.0 0.3 slice_add_fusion.2
  73.5 0.2 fusion.59
  74.3 7.8 %fusion.56 = (bf16[16,512,64]{1,2,0:T(8,128)(2,1)S(1)}, bf16[16,512,64]{1,2,0:T(8,128)(2,1)S(1)}) fusion(f32[512,64]{0,1:T(8,128)S(1)} %multiply_add_fusion.2, f32[16]{0:T(128)S(1)} %fusion.55), kind=kLoop, calls=%fused_computation.5.clone.1 | loop fusion | flops 1572864 | bytes 2228288 | tf_op jit(solution)/shard_map/convert
  82.1 0.4 fusion.57
  82.9 0.3 slice_add_fusion.2
  83.3 0.2 fusion.59
  84.2 7.8 %fusion.56 = (bf16[16,512,64]{1,2,0:T(8,128)(2,1)S(1)}, bf16[16,512,64]{1,2,0:T(8,128)(2,1)S(1)}) fusion(f32[512,64]{0,1:T(8,128)S(1)} %multiply_add_fusion.2, f32[16]{0:T(128)S(1)} %fusion.55), kind=kLoop, calls=%fused_computation.5.clone.1 | loop fusion | flops 1572864 | bytes 2228288 | tf_op jit(solution)/shard_map/convert
  92.0 0.4 fusion.57
  92.8 0.3 slice_add_fusion.2
  93.2 0.2 fusion.59
  94.1 7.8 %fusion.56 = (bf16[16,512,64]{1,2,0:T(8,128)(2,1)S(1)}, bf16[16,512,64]{1,2,0:T(8,128)(2,1)S(1)}) fusion(f32[512,64]{0,1:T(8,128)S(1)} %multiply_add_fusion.2, f32[16]{0:T(128)S(1)} %fusion.55), kind=kLoop, calls=%fused_computation.5.clone.1 | loop fusion | flops 1572864 | bytes 2228288 | tf_op jit(solution)/shard_map/convert
  101.8 0.4 fusion.57
  102.6 0.3 slice_add_fusion.2
  103.1 0.2 fusion.59
  103.9 7.8 %fusion.56 = (bf16[16,512,64]{1,2,0:T(8,128)(2,1)S(1)}, bf16[16,512,64]{1,2,0:T(8,128)(2,1)S(1)}) fusion(f32[512,64]{0,1:T(8,128)S(1)} %multiply_add_fusion.2, f32[16]{0:T(128)S(1)} %fusion.55), kind=kLoop, calls=%fused_computation.5.clone.1 | loop fusion | flops 1572864 | bytes 2228288 | tf_op jit(solution)/shard_map/convert
  111.7 0.4 fusion.57
  112.4 0.1 reshape.636
  112.5 0.3 slice_add_fusion.2
  112.9 0.2 fusion.59
  113.8 7.8 %fusion.56 = (bf16[16,512,64]{1,2,0:T(8,128)(2,1)S(1)}, bf16[16,512,64]{1,2,0:T(8,128)(2,1)S(1)}) fusion(f32[512,64]{0,1:T(8,128)S(1)} %multiply_add_fusion.2, f32[16]{0:T(128)S(1)} %fusion.55), kind=kLoop, calls=%fused_computation.5.clone.1 | loop fusion | flops 1572864 | bytes 2228288 | tf_op jit(solution)/shard_map/convert
  121.6 0.4 fusion.57
  122.1 0.1 reshape.635
  122.4 0.3 slice_add_fusion.2
  122.8 0.2 fusion.59
  123.6 7.8 %fusion.56 = (bf16[16,512,64]{1,2,0:T(8,128)(2,1)S(1)}, bf16[16,512,64]{1,2,0:T(8,128)(2,1)S(1)}) fusion(f32[512,64]{0,1:T(8,128)S(1)} %multiply_add_fusion.2, f32[16]{0:T(128)S(1)} %fusion.55), kind=kLoop, calls=%fused_computation.5.clone.1 | loop fusion | flops 1572864 | bytes 2228288 | tf_op jit(solution)/shard_map/convert
  131.4 0.4 fusion.57
  132.2 0.3 slice_add_fusion.2
  132.7 0.2 fusion.59
  133.2 0.6 copy-done.1
  (123 shorter events, 8.1 us)
Async XLA Ops:
  0.0 1.6 %copy-start = (bf16[64,2048]{1,0:T(8,128)(2,1)S(1)}, bf16[64,2048]{1,0:T(8,128)(2,1)}, u32[]{:S(2)}) copy-start(bf16[64,2048]{1,0:T(8,128)(2,1)} %param.6) | copy-start | bytes 786436
  3.0 14.2 %all-to-all-start = ((bf16[8,2,2048]{2,1,0:T(2,128)(2,1)}), bf16[8,2,2048]{2,1,0:T(2,128)(2,1)S(1)}, u32[]{:S(2)}, u32[]{:S(2)}) async-start(bf16[8,2,2048]{2,1,0:T(2,128)(2,1)} %broadcast_select_fusion.1), calls=%async_computation | async-start | bytes 131072 | tf_op jit(solution)/shard_map/all_to_all | solution.py:84
  33.5 13.4 %copy-start.2 = (s32[2,512]{1,0:T(2,128)S(1)}, s32[2,512]{1,0:T(2,128)}, u32[]{:S(2)}) copy-start(s32[2,512]{1,0:T(2,128)} %param.9) | copy-start | bytes 12292
  40.8 12.9 %all-to-all-start.1 = ((bf16[8,2,4096]{2,1,0:T(2,128)(2,1)}), bf16[8,2,4096]{2,1,0:T(2,128)(2,1)S(1)}, u32[]{:S(2)}, u32[]{:S(2)}) async-start(bf16[8,2,4096]{2,1,0:T(2,128)(2,1)} %reshape.631), calls=%async_computation.1 | async-start | bytes 262144 | tf_op jit(solution)/shard_map/all_to_all | solution.py:112
  133.2 0.6 copy-start.1
where the time goes:
time: 134 us
  other arithmetic  78 us (58%)
  local copies, waits for them, and re-layouts  24.5 us (18%)
  starting transfers between devices  12.6 us (9%)
  waiting for transfers between devices  7.29 us (5%)
  blocking collectives  5.78 us (4%)
  matrix products  3.81 us (3%)
    another operation x9, other arithmetic  63 us
    reshape x1, local copies, waits for them, and re-layouts, per_device(): (spectral * dft_scale).astype(jnp.bfloat16)  9.98 us
    all_to_all x1, starting transfers between devices, per_device(): lax.all_to_all(packed, 'vol', split_axis=0, concat_axis=0, tiled=True)  7.28 us
    all_to_all x1, waiting for transfers between devices, per_device(): lax.all_to_all(spectra, 'vol', split_axis=0, concat_axis=2, tiled=True)  6.64 us
    transpose x1, local copies, waits for them, and re-layouts, per_device(): spectra = spectral.transpose(2, 1, 3, 0).reshape(bin_cap, 2 * NQ, rows_here)  6.2 us
    all_gather x1, blocking collectives, per_device(): row_piece = lax.all_gather(arrived, 'nar', axis=0, tiled=True)  5.78 us
    all_to_all x1, starting transfers between devices, per_device(): lax.all_to_all(spectra, 'vol', split_axis=0, concat_axis=2, tiled=True)  5.37 us
    dot_general x8, matrix products, apply_green(): jnp.einsum('bxp,bcp->bxc', green_grid, spec_block, preferred_element_type...  3.55 us
  transfers between devices with their start and end apart: 2, of which 2 were waited for; matrix products, arithmetic and copies ran while one was open for 5% of the time, Pallas kernels for 0%

commit v1 on v0

--- a/solution.py
+++ b/solution.py
@@ -7,6 +7,28 @@
 NF = 256
 NQ = 4
 WAVE_STEP = 0.05
+
+
+def cut_along(array, dim, size):
+    before, after = (array.shape[:dim], array.shape[dim + 1 :])
+    return jnp.moveaxis(array.reshape(*before, size, -1, *after), dim, 0)
+
+
+def in_order(blocks, dim):
+    blocks = jnp.moveaxis(blocks, 0, dim)
+    lengths = blocks.shape
+    return blocks.reshape(*lengths[:dim], lengths[dim] * lengths[dim + 1], *lengths[dim + 2 :])
+
+
+def sent_to_each(array, axis, split_dim, concat_dim):
+    devices, position = (lax.axis_size(axis), lax.axis_index(axis))
+    blocks = cut_along(array, split_dim, devices)
+    done = [blocks[position]]
+    for turn in range(1, devices):
+        sent = blocks[(position + turn) % devices]
+        done.append(lax.ppermute(sent, axis, [(i, (i + turn) % devices) for i in range(devices)]))
+    blocks = jnp.stack(done)[(position - jnp.arange(devices)) % devices]
+    return in_order(blocks, concat_dim)
 
 
 def dft_table(bin_ids, keep_bin, time_len):
@@ -81,7 +103,7 @@
     listing = send_rows.reshape(-1)
     picked = jnp.take(series, jnp.maximum(listing, 0), axis=0)
     packed = jnp.where((listing >= 0)[:, None], picked, jnp.zeros((), series.dtype))
-    arrived = lax.all_to_all(packed, "vol", split_axis=0, concat_axis=0, tiled=True)
+    arrived = sent_to_each(packed, "vol", 0, 0)
     starts = jnp.cumsum(bin_counts) - bin_counts
     own_start = starts[nar_index]
     own_count = bin_counts[nar_index]

time: 134 us -> 143 us (1.067)
  starting transfers between devices: 12.6 us -> 19.3 us
  waiting for transfers between devices: 7.29 us -> 8.85 us
    ppermute x0 -> x7, starting transfers between devices: none -> 13.9 us  [sent_to_each(): lax.ppermute(sent, axis, [(i, (i + turn) % devices) for i in range(device...]
    all_to_all x1 -> x0, starting transfers between devices: 7.28 us -> none  [per_device(): lax.all_to_all(packed, 'vol', split_axis=0, concat_axis=0, tiled=True)]
    ppermute x0 -> x7, waiting for transfers between devices: none -> 2.11 us  [sent_to_each(): lax.ppermute(sent, axis, [(i, (i + turn) % devices) for i in range(device...]
  transfers between devices with their start and end apart: 2 -> 8, of which waited for: 2 -> 3; matrix products, arithmetic and copies ran while one was open for 5% -> 4% of each run, Pallas kernels for 0% -> 0%
where the time goes in v1:
time: 143 us; the launch traced here: 142 us
  other arithmetic  77.3 us (54%)
  local copies, waits for them, and re-layouts  25.3 us (18%)
  starting transfers between devices  19.3 us (13%)
  waiting for transfers between devices  8.85 us (6%)
  blocking collectives  5.78 us (4%)
  matrix products  3.81 us (3%)
    another operation x9, other arithmetic  63 us
    ppermute x7, starting transfers between devices, sent_to_each(): lax.ppermute(sent, axis, [(i, (i + turn) % devices) for i in range(device...  13.9 us
    reshape x1, local copies, waits for them, and re-layouts, per_device(): (spectral * dft_scale).astype(jnp.bfloat16)  9.98 us
    all_to_all x1, waiting for transfers between devices, per_device(): lax.all_to_all(spectra, 'vol', split_axis=0, concat_axis=2, tiled=True)  6.74 us
    transpose x1, local copies, waits for them, and re-layouts, per_device(): spectra = spectral.transpose(2, 1, 3, 0).reshape(bin_cap, 2 * NQ, rows_here)  6.2 us
    all_gather x1, blocking collectives, per_device(): row_piece = lax.all_gather(arrived, 'nar', axis=0, tiled=True)  5.78 us
    all_to_all x1, starting transfers between devices, per_device(): lax.all_to_all(spectra, 'vol', split_axis=0, concat_axis=2, tiled=True)  5.4 us
    dot_general x8, matrix products, apply_green(): jnp.einsum('bxp,bcp->bxc', green_grid, spec_block, preferred_element_type...  3.55 us
  transfers between devices with their start and end apart: 8, of which 3 were waited for; matrix products, arithmetic and copies ran while one was open for 4% of the time, Pallas kernels for 0%

profile of v1, /device:TPU:0, one launch (start us, length us, event | category | flops | bytes accessed | tf_op | source)
XLA Modules:
  0.0 142.2 jit_solution(1380495788933760546)
XLA Ops:
  0.0 0.7 compare_reduce_fusion
  0.7 0.7 maximum_bitcast_fusion
  1.6 0.6 gather_fusion
  2.5 3.0 %collective-permute-start = (bf16[2,2048]{1,0:T(2,128)(2,1)S(1)}, bf16[2,2048]{1,0:T(2,128)(2,1)S(1)}, u32[]{:S(2)}, u32[]{:S(2)}) collective-permute-start(bf16[2,2048]{1,0:T(2,128)(2,1)S(1)} %get-tuple-element.355), channel_id=1, source_target_pairs={{0,4},{4,8},{8,12},{12,16},{16,20},{20,24},{24,28},{28,0},{1,5},{5... | collective-permute-start | bytes 24584 | tf_op jit(solution)/shard_map/ppermute | solution.py:29
  5.5 1.6 %collective-permute-start.1 = (bf16[2,2048]{1,0:T(2,128)(2,1)S(1)}, bf16[2,2048]{1,0:T(2,128)(2,1)S(1)}, u32[]{:S(2)}, u32[]{:S(2)}) collective-permute-start(bf16[2,2048]{1,0:T(2,128)(2,1)S(1)} %get-tuple-element.354), channel_id=1, source_target_pairs={{0,8},{4,12},{8,16},{12,20},{16,24},{20,28},{24,0},{28,4},{1,9},{5... | collective-permute-start | bytes 24584 | tf_op jit(solution)/shard_map/ppermute | solution.py:29
  7.1 2.6 %collective-permute-start.2 = (bf16[2,2048]{1,0:T(2,128)(2,1)S(1)}, bf16[2,2048]{1,0:T(2,128)(2,1)S(1)}, u32[]{:S(2)}, u32[]{:S(2)}) collective-permute-start(bf16[2,2048]{1,0:T(2,128)(2,1)S(1)} %get-tuple-element.353), channel_id=1, source_target_pairs={{0,12},{4,16},{8,20},{12,24},{16,28},{20,0},{24,4},{28,8},{1,13},{... | collective-permute-start | bytes 24584 | tf_op jit(solution)/shard_map/ppermute | solution.py:29
  9.7 1.2 collective-permute-start.3
  10.9 2.6 %collective-permute-start.4 = (bf16[2,2048]{1,0:T(2,128)(2,1)S(1)}, bf16[2,2048]{1,0:T(2,128)(2,1)S(1)}, u32[]{:S(2)}, u32[]{:S(2)}) collective-permute-start(bf16[2,2048]{1,0:T(2,128)(2,1)S(1)} %get-tuple-element.351), channel_id=1, source_target_pairs={{0,20},{4,24},{8,28},{12,0},{16,4},{20,8},{24,12},{28,16},{1,21},{... | collective-permute-start | bytes 24584 | tf_op jit(solution)/shard_map/ppermute | solution.py:29
  13.5 0.8 reduce-window.9
  14.4 0.7 bitcast_subtract_fusion
  15.0 1.2 dynamic_slice.50
  16.2 0.6 dynamic_slice.41
  16.9 0.6 add_add_fusion
  17.5 1.1 fusion.36
  18.6 0.7 iota_compare_fusion
  19.7 1.4 collective-permute-start.5
  21.1 1.5 %collective-permute-start.6 = (bf16[2,2048]{1,0:T(2,128)(2,1)S(1)}, bf16[2,2048]{1,0:T(2,128)(2,1)S(1)}, u32[]{:S(2)}, u32[]{:S(2)}) collective-permute-start(bf16[2,2048]{1,0:T(2,128)(2,1)S(1)} %get-tuple-element.349), channel_id=1, source_target_pairs={{0,28},{4,0},{8,4},{12,8},{16,12},{20,16},{24,20},{28,24},{1,29},{... | collective-permute-start | bytes 24584 | tf_op jit(solution)/shard_map/ppermute | solution.py:29
  22.7 0.7 collective-permute-done.5
  23.4 1.4 collective-permute-done.6
  24.8 0.7 gather_fusion.1
  25.5 5.8 %all_gather.3 = bf16[64,2048]{1,0:T(8,128)(2,1)S(1)} all-gather(bf16[16,2048]{1,0:T(8,128)(2,1)S(1)} %reshape.648), channel_id=1, replica_groups=mesh['vol'=8,'nar'=4] {'nar'}, dimensions={0}, use_global_device_ids=true | all-gather | bytes 327680 | tf_op jit(solution)/shard_map/all_gather | solution.py:113
  31.5 0.3 fusion.28
  31.8 10.0 %reshape.650 = bf16[64,4,128,2]{1,0,3,2:T(8,128)(2,1)} reshape(bf16[256,256]{0,1:T(8,128)(2,1)S(1)} %copy.27) | data formatting | bytes 262144 | tf_op jit(solution)/shard_map/reshape | solution.py:118
  41.8 6.2 %copy.28 = bf16[128,4,2,64]{0,3,2,1:T(8,128)(2,1)S(1)} copy(bf16[128,4,2,64]{1,3,2,0:T(8,128)(2,1)} %bitcast.94) | data formatting | bytes 262144 | tf_op jit(solution)/shard_map/transpose | solution.py:119
  48.0 0.2 copy.29
  48.2 0.9 reshape.691
  49.1 5.4 %all-to-all-start = ((bf16[8,2,4096]{2,1,0:T(2,128)(2,1)}), bf16[8,2,4096]{2,1,0:T(2,128)(2,1)S(1)}, u32[]{:S(2)}, u32[]{:S(2)}) async-start(bf16[8,2,4096]{2,1,0:T(2,128)(2,1)} %reshape.691), calls=%async_computation | async-start | bytes 262144 | tf_op jit(solution)/shard_map/all_to_all | solution.py:134
  55.3 6.7 %all-to-all-done = bf16[8,2,4096]{2,1,0:T(2,128)(2,1)S(1)} async-done(((bf16[8,2,4096]{2,1,0:T(2,128)(2,1)}), bf16[8,2,4096]{2,1,0:T(2,128)(2,1)S(1)}, u32[]{:S(2)}, u32[]{:S(2)}) %all-to-all-start) | async-done | bytes 131104 | tf_op jit(solution)/shard_map/all_to_all | solution.py:134
  62.0 0.2 reshape.692
  62.4 0.2 all_to_all.16
  62.6 78.9 %while.19 = (s32[]{:T(128)}, f32[16,2,512]{2,1,0:T(2,128)S(1)}, f32[512]{0:T(512)S(1)}, f32[512]{0:T(512)S(1)}, f32[512]{0:T(512)S(1)}, /*index=5*/bf16[16,8,512...) while((s32[]{:T(128)}, f32[16,2,512]{2,1,0:T(2,128)S(1)}, ...), condition=%wide.region_4.5_spmd.clone.clone.clone, body=%wide.region_1.4_spmd.clone.clone.clone.sunk | while | flops 22971540 | bytes 8845429 | solution.py:147
  63.0 7.8 %fusion.58 = (bf16[16,512,64]{1,2,0:T(8,128)(2,1)S(1)}, bf16[16,512,64]{1,2,0:T(8,128)(2,1)S(1)}) fusion(f32[512,64]{0,1:T(8,128)S(1)} %multiply_add_fusion.2, f32[16]{0:T(128)S(1)} %fusion.57), kind=kLoop, calls=%fused_computation.6.clone.1 | loop fusion | flops 1572864 | bytes 2228288 | tf_op jit(solution)/shard_map/convert
  70.8 0.4 fusion.59
  71.6 0.3 slice_add_fusion.2
  72.0 0.2 fusion.61
  72.8 7.8 %fusion.58 = (bf16[16,512,64]{1,2,0:T(8,128)(2,1)S(1)}, bf16[16,512,64]{1,2,0:T(8,128)(2,1)S(1)}) fusion(f32[512,64]{0,1:T(8,128)S(1)} %multiply_add_fusion.2, f32[16]{0:T(128)S(1)} %fusion.57), kind=kLoop, calls=%fused_computation.6.clone.1 | loop fusion | flops 1572864 | bytes 2228288 | tf_op jit(solution)/shard_map/convert
  80.6 0.4 fusion.59
  81.4 0.3 slice_add_fusion.2
  81.9 0.2 fusion.61
  82.7 7.8 %fusion.58 = (bf16[16,512,64]{1,2,0:T(8,128)(2,1)S(1)}, bf16[16,512,64]{1,2,0:T(8,128)(2,1)S(1)}) fusion(f32[512,64]{0,1:T(8,128)S(1)} %multiply_add_fusion.2, f32[16]{0:T(128)S(1)} %fusion.57), kind=kLoop, calls=%fused_computation.6.clone.1 | loop fusion | flops 1572864 | bytes 2228288 | tf_op jit(solution)/shard_map/convert
  90.5 0.4 fusion.59
  91.3 0.3 slice_add_fusion.2
  91.7 0.2 fusion.61
  92.6 7.8 %fusion.58 = (bf16[16,512,64]{1,2,0:T(8,128)(2,1)S(1)}, bf16[16,512,64]{1,2,0:T(8,128)(2,1)S(1)}) fusion(f32[512,64]{0,1:T(8,128)S(1)} %multiply_add_fusion.2, f32[16]{0:T(128)S(1)} %fusion.57), kind=kLoop, calls=%fused_computation.6.clone.1 | loop fusion | flops 1572864 | bytes 2228288 | tf_op jit(solution)/shard_map/convert
  100.4 0.4 fusion.59
  101.2 0.3 slice_add_fusion.2
  101.6 0.2 fusion.61
  102.4 7.8 %fusion.58 = (bf16[16,512,64]{1,2,0:T(8,128)(2,1)S(1)}, bf16[16,512,64]{1,2,0:T(8,128)(2,1)S(1)}) fusion(f32[512,64]{0,1:T(8,128)S(1)} %multiply_add_fusion.2, f32[16]{0:T(128)S(1)} %fusion.57), kind=kLoop, calls=%fused_computation.6.clone.1 | loop fusion | flops 1572864 | bytes 2228288 | tf_op jit(solution)/shard_map/convert
  110.2 0.4 fusion.59
  111.0 0.3 slice_add_fusion.2
  111.5 0.2 fusion.61
  112.3 7.8 %fusion.58 = (bf16[16,512,64]{1,2,0:T(8,128)(2,1)S(1)}, bf16[16,512,64]{1,2,0:T(8,128)(2,1)S(1)}) fusion(f32[512,64]{0,1:T(8,128)S(1)} %multiply_add_fusion.2, f32[16]{0:T(128)S(1)} %fusion.57), kind=kLoop, calls=%fused_computation.6.clone.1 | loop fusion | flops 1572864 | bytes 2228288 | tf_op jit(solution)/shard_map/convert
  120.1 0.4 fusion.59
  120.9 0.3 slice_add_fusion.2
  121.3 0.2 fusion.61
  122.2 7.8 %fusion.58 = (bf16[16,512,64]{1,2,0:T(8,128)(2,1)S(1)}, bf16[16,512,64]{1,2,0:T(8,128)(2,1)S(1)}) fusion(f32[512,64]{0,1:T(8,128)S(1)} %multiply_add_fusion.2, f32[16]{0:T(128)S(1)} %fusion.57), kind=kLoop, calls=%fused_computation.6.clone.1 | loop fusion | flops 1572864 | bytes 2228288 | tf_op jit(solution)/shard_map/convert
  130.0 0.4 fusion.59
  130.8 0.3 slice_add_fusion.2
  131.2 0.2 fusion.61
  132.0 7.8 %fusion.58 = (bf16[16,512,64]{1,2,0:T(8,128)(2,1)S(1)}, bf16[16,512,64]{1,2,0:T(8,128)(2,1)S(1)}) fusion(f32[512,64]{0,1:T(8,128)S(1)} %multiply_add_fusion.2, f32[16]{0:T(128)S(1)} %fusion.57), kind=kLoop, calls=%fused_computation.6.clone.1 | loop fusion | flops 1572864 | bytes 2228288 | tf_op jit(solution)/shard_map/convert
  139.8 0.4 fusion.59
  140.6 0.3 slice_add_fusion.2
  141.1 0.2 fusion.61
  141.6 0.6 copy-done.1
  (146 shorter events, 9.6 us)
Async XLA Ops:
  0.0 1.6 %copy-start = (bf16[64,2048]{1,0:T(8,128)(2,1)S(1)}, bf16[64,2048]{1,0:T(8,128)(2,1)}, u32[]{:S(2)}) copy-start(bf16[64,2048]{1,0:T(8,128)(2,1)} %param.6) | copy-start | bytes 786436
  2.5 17.2 %collective-permute-start = (bf16[2,2048]{1,0:T(2,128)(2,1)S(1)}, bf16[2,2048]{1,0:T(2,128)(2,1)S(1)}, u32[]{:S(2)}, u32[]{:S(2)}) collective-permute-start(bf16[2,2048]{1,0:T(2,128)(2,1)S(1)} %get-tuple-element.355), channel_id=1, source_target_pairs={{0,4},{4,8},{8,12},{12,16},{16,20},{20,24},{24,28},{28,0},{1,5},{5... | collective-permute-start | bytes 24584 | tf_op jit(solution)/shard_map/ppermute | solution.py:29
  5.5 15.6 %collective-permute-start.1 = (bf16[2,2048]{1,0:T(2,128)(2,1)S(1)}, bf16[2,2048]{1,0:T(2,128)(2,1)S(1)}, u32[]{:S(2)}, u32[]{:S(2)}) collective-permute-start(bf16[2,2048]{1,0:T(2,128)(2,1)S(1)} %get-tuple-element.354), channel_id=1, source_target_pairs={{0,8},{4,12},{8,16},{12,20},{16,24},{20,28},{24,0},{28,4},{1,9},{5... | collective-permute-start | bytes 24584 | tf_op jit(solution)/shard_map/ppermute | solution.py:29
  7.1 15.5 %collective-permute-start.2 = (bf16[2,2048]{1,0:T(2,128)(2,1)S(1)}, bf16[2,2048]{1,0:T(2,128)(2,1)S(1)}, u32[]{:S(2)}, u32[]{:S(2)}) collective-permute-start(bf16[2,2048]{1,0:T(2,128)(2,1)S(1)} %get-tuple-element.353), channel_id=1, source_target_pairs={{0,12},{4,16},{8,20},{12,24},{16,28},{20,0},{24,4},{28,8},{1,13},{... | collective-permute-start | bytes 24584 | tf_op jit(solution)/shard_map/ppermute | solution.py:29
  9.7 13.0 %collective-permute-start.3 = (bf16[2,2048]{1,0:T(2,128)(2,1)S(1)}, bf16[2,2048]{1,0:T(2,128)(2,1)S(1)}, u32[]{:S(2)}, u32[]{:S(2)}) collective-permute-start(bf16[2,2048]{1,0:T(2,128)(2,1)S(1)} %get-tuple-element.352), channel_id=1, source_target_pairs={{0,16},{4,20},{8,24},{12,28},{16,0},{20,4},{24,8},{28,12},{1,17},{... | collective-permute-start | bytes 24584 | tf_op jit(solution)/shard_map/ppermute | solution.py:29
  10.9 11.8 %collective-permute-start.4 = (bf16[2,2048]{1,0:T(2,128)(2,1)S(1)}, bf16[2,2048]{1,0:T(2,128)(2,1)S(1)}, u32[]{:S(2)}, u32[]{:S(2)}) collective-permute-start(bf16[2,2048]{1,0:T(2,128)(2,1)S(1)} %get-tuple-element.351), channel_id=1, source_target_pairs={{0,20},{4,24},{8,28},{12,0},{16,4},{20,8},{24,12},{28,16},{1,21},{... | collective-permute-start | bytes 24584 | tf_op jit(solution)/shard_map/ppermute | solution.py:29
  19.7 3.7 %collective-permute-start.5 = (bf16[2,2048]{1,0:T(2,128)(2,1)S(1)}, bf16[2,2048]{1,0:T(2,128)(2,1)S(1)}, u32[]{:S(2)}, u32[]{:S(2)}) collective-permute-start(bf16[2,2048]{1,0:T(2,128)(2,1)S(1)} %get-tuple-element.350), channel_id=1, source_target_pairs={{0,24},{4,28},{8,0},{12,4},{16,8},{20,12},{24,16},{28,20},{1,25},{... | collective-permute-start | bytes 24584 | tf_op jit(solution)/shard_map/ppermute | solution.py:29
  21.1 3.7 %collective-permute-start.6 = (bf16[2,2048]{1,0:T(2,128)(2,1)S(1)}, bf16[2,2048]{1,0:T(2,128)(2,1)S(1)}, u32[]{:S(2)}, u32[]{:S(2)}) collective-permute-start(bf16[2,2048]{1,0:T(2,128)(2,1)S(1)} %get-tuple-element.349), channel_id=1, source_target_pairs={{0,28},{4,0},{8,4},{12,8},{16,12},{20,16},{24,20},{28,24},{1,29},{... | collective-permute-start | bytes 24584 | tf_op jit(solution)/shard_map/ppermute | solution.py:29
  41.8 13.3 %copy-start.2 = (s32[2,512]{1,0:T(2,128)S(1)}, s32[2,512]{1,0:T(2,128)}, u32[]{:S(2)}) copy-start(s32[2,512]{1,0:T(2,128)} %param.9) | copy-start | bytes 12292
  49.1 12.9 %all-to-all-start = ((bf16[8,2,4096]{2,1,0:T(2,128)(2,1)}), bf16[8,2,4096]{2,1,0:T(2,128)(2,1)S(1)}, u32[]{:S(2)}, u32[]{:S(2)}) async-start(bf16[8,2,4096]{2,1,0:T(2,128)(2,1)} %reshape.691), calls=%async_computation | async-start | bytes 262144 | tf_op jit(solution)/shard_map/all_to_all | solution.py:134
  141.6 0.6 copy-start.1
